TPU v7x, 32 devices: a whole 2x2x4 slice. The times are simulated.
32 devices in a mesh: dp: 16 (over z, x, core), rep: 2 (over y).
Axes of the slice: x: 2, y: 2, z: 4, core: 2. Of those that a mesh axis runs over, the one named last changes fastest.
Arguments:
- grad_out: bfloat16 [12288, 2048], P('dp', 'rep'), may hold values from -6 to 6
- pre_act: bfloat16 [12288, 3072], P('dp', 'rep'), may hold values from -6 to 6
- up_weight: bfloat16 [3072, 2048], P('rep'), may hold values from -0.125 to 0.125
- down_weight: bfloat16 [2048, 3072], P(None, 'rep'), may hold values from -0.109375 to 0.109375
- slot_counts: int32 [16], P('dp'), may hold values from 384 to 768, as said below
Outputs:
- input_grad: bfloat16 [12288, 2048], P('dp')
- down_grad: float32 [2048, 3072], P('dp', 'rep')
Inputs may be any that keep to these rules, and one draw needn't show every extreme that they name: Row i * 768 + j is live exactly when j < slot_counts[i]; some index has all 768 slots live and some index exactly 384.
All inputs are finite; a program needn't handle non-finite values.
Results may differ from a plain program's by a relative error of at most 0.0049.
Values may be sent and summed in bfloat16 or wider, within the bound.
A program may use at most 128 MiB of HBM per device.

v0:
```python
import jax
import jax.numpy as jnp
from jax import lax
from jax.sharding import PartitionSpec as P


def on_device(grad_out, pre_act, up_weight, down_weight, slot_counts):
    slot_rows = grad_out.shape[0]
    live_rows = (lax.iota(jnp.int32, slot_rows) < slot_counts[0])[:, None]
    grad_full = lax.all_gather(grad_out, "rep", axis=1, tiled=True)
    grad_live = jnp.where(live_rows, grad_full, jnp.zeros_like(grad_full))
    zero_pre = jnp.zeros_like(pre_act)
    hidden = jnp.where(live_rows, jnp.maximum(pre_act, zero_pre), zero_pre)
    data_ranks = lax.axis_size("dp")
    down_sum = lax.psum_scatter(
        lax.dot_general(
            grad_live, hidden, (((0,), (0,)), ((), ())), preferred_element_type=jnp.float32
        ),
        "dp",
        scatter_dimension=0,
        tiled=True,
    )
    down_grad = down_sum / data_ranks
    hidden_grad = jnp.dot(grad_live, down_weight, preferred_element_type=jnp.float32)
    pre_grad = jnp.where(pre_act > 0, hidden_grad, jnp.zeros_like(hidden_grad)).astype(jnp.bfloat16)
    partial_terms = jnp.dot(pre_grad, up_weight, preferred_element_type=jnp.float32)
    input_sum = lax.psum(partial_terms, "rep")
    input_grad = input_sum.astype(jnp.bfloat16)
    return (input_grad, down_grad)


def solution(mesh):
    return jax.shard_map(
        on_device,
        mesh=mesh,
        in_specs=(P("dp", "rep"), P("dp", "rep"), P("rep", None), P(None, "rep"), P("dp")),
        out_specs=(P("dp", None), P("dp", "rep")),
        check_vma=False,
    )
```

profile of v0, /device:TPU:0, one launch (start us, length us, event | category | flops | bytes accessed | tf_op | source)
XLA Modules:
  0.0 245.0 jit_solution(6977455939318011038)
XLA Ops:
  7.2 0.0 all-gather.2.cloned.1.call-start
  7.2 0.7 all-gather.2.cloned.1.call-update
  7.9 0.0 reduce-scatter.2.cloned.1.call-start
  8.6 48.6 %all-gather.2.cloned.1.call-done = bf16[768,2048]{1,0:T(8,128)(2,1)} async-done(((bf16[768,1024]{1,0:T(8,128)(2,1)}), bf16[768,2048]{1,0:T(8,128)(2,1)}) %all-gather.2.cloned.1.call-update) | async-done | bytes 3145744 | tf_op jit(solution)/shard_map/all_gather | solution.py:10
  57.2 10.7 %fusion = f32[2048,1536]{1,0:T(8,128)} fusion(bf16[768,1536]{1,0:T(8,128)(2,1)} %param.6, pred[768]{0:T(1024)(128)(4,1)S(1)} %iota_compare_fusion, bf16[768,2048]{1,0:T(8,128)(2,1)} %all-gather.2.cloned.1.call-done), kind=kOutput, calls=%fused_computation.2 | convolution fusion | flops 4835770368 | bytes 18088704 | tf_op jit(solution)/shard_map/dot_general | solution.py:16
  67.9 0.0 copy-start
  67.9 0.0 reduce-scatter.2.cloned.1.call-update
  67.9 1.9 copy-done
  69.8 19.0 %fusion.5 = f32[768,2048]{1,0:T(8,128)} fusion(bf16[1536,2048]{1,0:T(8,128)(2,1)} %param.7, bf16[768,1536]{1,0:T(8,128)(2,1)} %param.6, bf16[2048,1536]{1,0:T(8,128)(2,1)} %param.8, bf16[768,2048]{1,0:T(8,128)(2,1)S(1)} %copy-done, pred[768]{0:T(1024)(128)(4,1)S(1)} %iota_compare_fusion), kind=kOutput, calls=%fused_computation.7 | convolution fusion | flops 9668788224 | bytes 24380160 | tf_op jit(solution)/shard_map/dot_general | solution.py:26
  88.8 147.3 %all-reduce.1 = bf16[768,2048]{1,0:T(8,128)(2,1)} all-reduce(f32[768,2048]{1,0:T(8,128)} %fusion.5), channel_id=1, replica_groups=mesh['dp'=16,'rep'=2] {'rep'}, use_global_device_ids=true, to_apply=%region_0.1 | all-reduce | flops 1572864 | bytes 9437184 | tf_op jit(solution)/shard_map/psum | solution.py:27
  236.1 0.0 reduce-scatter.2.cloned.1.call-done
  236.1 2.1 broadcast_multiply_fusion
  (1 shorter events, 0.0 us)
Async XLA Ops:
  7.2 50.0 %all-gather.2.cloned.1.call-start = ((), (), s32[]{:S(2)}) async-start(), calls=%async_computation.1 | async-start | bytes 4718592 | tf_op jit(solution)/shard_map/all_gather | solution.py:10
  7.9 228.2 %reduce-scatter.2.cloned.1.call-start = ((), (), s32[]{:S(2)}) async-start(), calls=%async_computation.2 | async-start | bytes 13369344 | tf_op jit(solution)/shard_map/reduce_scatter | solution.py:15
  67.9 1.9 copy-start
Sparse Core Ops, SparseCore 0:
  9.5 47.6 all-gather.1
  68.1 134.9 reduce-scatter.1
where the time goes:
time: 245 us
  blocking collectives  147 us (60%)
  waiting for transfers between devices  49.3 us (20%)
  matrix products  29.7 us (12%)
  between operations  14.7 us (6%)
    psum x1, blocking collectives, on_device(): input_sum = lax.psum(partial_terms, 'rep')  147 us
    all_gather x1, waiting for transfers between devices, on_device(): grad_full = lax.all_gather(grad_out, 'rep', axis=1, tiled=True)  48.6 us
    dot_general x1, matrix products, on_device(): jnp.dot(pre_grad, up_weight, preferred_element_type=jnp.float32)  19 us
    dot_general x1, matrix products, on_device(): lax.dot_general(grad_live, hidden, (((0,), (0,)), ((), ())), preferred_el...  10.7 us
  transfers between devices with their start and end apart: 2, of which 1 were waited for; matrix products, arithmetic and copies ran while one was open for 8% of the time, Pallas kernels for 0%

commit v1 on v0

--- a/solution.py
+++ b/solution.py
@@ -24,7 +24,7 @@
     hidden_grad = jnp.dot(grad_live, down_weight, preferred_element_type=jnp.float32)
     pre_grad = jnp.where(pre_act > 0, hidden_grad, jnp.zeros_like(hidden_grad)).astype(jnp.bfloat16)
     partial_terms = jnp.dot(pre_grad, up_weight, preferred_element_type=jnp.float32)
-    input_sum = lax.psum(partial_terms, "rep")
+    input_sum = lax.all_gather(partial_terms, axis_name="rep").sum(axis=0)
     input_grad = input_sum.astype(jnp.bfloat16)
     return (input_grad, down_grad)
 

time: 245 us -> 377 us (1.54)
  waiting for transfers between devices: 49.3 us -> 319 us
  blocking collectives: 147 us -> 0 us
  other arithmetic: 2.08 us -> 10.6 us
    psum x1 -> x0, blocking collectives: 147 us -> none  [on_device(): input_sum = lax.psum(partial_terms, 'rep')]
    all_gather x0 -> x1, waiting for transfers between devices: none -> 139 us  [on_device(): input_sum = lax.all_gather(partial_terms, axis_name='rep').sum(axis=0)]
    reduce_scatter x1, waiting for transfers between devices: 0.01 us -> 131 us  [on_device(): lax.psum_scatter(lax.dot_general(grad_live, hidden, (((0,), (0,)), ((), (...]
    reduce_sum x0 -> x1, other arithmetic: none -> 8.5 us  [on_device(): input_sum = lax.all_gather(partial_terms, axis_name='rep').sum(axis=0)]
  transfers between devices with their start and end apart: 2 -> 3, of which waited for: 1 -> 3; matrix products, arithmetic and copies ran while one was open for 8% -> 5% of each run, Pallas kernels for 0% -> 0%
where the time goes in v1:
time: 377 us; the launch traced here: 376 us
  waiting for transfers between devices  319 us (85%)
  matrix products  31 us (8%)
  between operations  14.4 us (4%)
  other arithmetic  10.6 us (3%)
    all_gather x1, waiting for transfers between devices, on_device(): input_sum = lax.all_gather(partial_terms, axis_name='rep').sum(axis=0)  139 us
    reduce_scatter x1, waiting for transfers between devices, on_device(): lax.psum_scatter(lax.dot_general(grad_live, hidden, (((0,), (0,)), ((), (...  131 us
    all_gather x1, waiting for transfers between devices, on_device(): grad_full = lax.all_gather(grad_out, 'rep', axis=1, tiled=True)  48.6 us
    dot_general x1, matrix products, on_device(): jnp.dot(pre_grad, up_weight, preferred_element_type=jnp.float32)  19 us
    dot_general x1, matrix products, on_device(): lax.dot_general(grad_live, hidden, (((0,), (0,)), ((), ())), preferred_el...  12 us
    reduce_sum x1, other arithmetic, on_device(): input_sum = lax.all_gather(partial_terms, axis_name='rep').sum(axis=0)  8.5 us
  transfers between devices with their start and end apart: 3, of which 3 were waited for; matrix products, arithmetic and copies ran while one was open for 5% of the time, Pallas kernels for 0%

profile of v1, /device:TPU:0, one launch (start us, length us, event | category | flops | bytes accessed | tf_op | source)
XLA Modules:
  0.0 376.4 jit_solution(8060342732184660241)
XLA Ops:
  7.2 0.0 all-gather.4.cloned.1.call-start
  7.2 0.7 all-gather.4.cloned.1.call-update
  7.9 0.0 all-gather.6.cloned.1.call-start
  8.6 48.6 %all-gather.4.cloned.1.call-done = bf16[768,2048]{1,0:T(8,128)(2,1)} async-done(((bf16[768,1024]{1,0:T(8,128)(2,1)}), bf16[768,2048]{1,0:T(8,128)(2,1)}) %all-gather.4.cloned.1.call-update) | async-done | bytes 3145744 | tf_op jit(solution)/shard_map/all_gather | solution.py:10
  57.2 19.0 %fusion.5 = f32[768,2048]{1,0:T(8,128)} fusion(bf16[1536,2048]{1,0:T(8,128)(2,1)} %param.7, bf16[768,1536]{1,0:T(8,128)(2,1)} %param.6, bf16[2048,1536]{1,0:T(8,128)(2,1)} %param.8, bf16[768,2048]{1,0:T(8,128)(2,1)} %all-gather.4.cloned.1.call-done, pred[768]{0:T(1024)(128)(4,1)S(1)} %iota_compare_fusion), kind=kOutput, calls=%fused_computation.7 | convolution fusion | flops 9668788224 | bytes 24380160 | tf_op jit(solution)/shard_map/dot_general | solution.py:26
  76.1 0.0 copy-start
  76.1 0.0 all-gather.6.cloned.1.call-update
  76.2 0.0 reduce-scatter.2.cloned.1.call-start
  76.2 1.8 copy-done
  78.0 12.0 %fusion = f32[2048,1536]{1,0:T(8,128)} fusion(bf16[768,1536]{1,0:T(8,128)(2,1)} %param.6, pred[768]{0:T(1024)(128)(4,1)S(1)} %iota_compare_fusion, bf16[768,2048]{1,0:T(8,128)(2,1)S(1)} %copy-done), kind=kOutput, calls=%fused_computation.2 | convolution fusion | flops 4835770368 | bytes 18088704 | tf_op jit(solution)/shard_map/dot_general | solution.py:16
  90.0 0.0 reduce-scatter.2.cloned.1.call-update
  90.1 138.8 %all-gather.6.cloned.1.call-done = f32[1536,2048]{1,0:T(8,128)} async-done(((f32[768,2048]{1,0:T(8,128)}), f32[1536,2048]{1,0:T(8,128)}) %all-gather.6.cloned.1.call-update) | async-done | bytes 12582928 | tf_op jit(solution)/shard_map/all_gather | solution.py:27
  228.8 8.5 %reduce_sum.9 = bf16[768,2048]{1,0:T(8,128)(2,1)} reduce(f32[2,768,2048]{2,1,0:T(8,128)} %bitcast.5, f32[]{:T(128)} %constant.4.clone.1), dimensions={0}, to_apply=%region_0.1 | reduce | flops 1572864 | bytes 15728644 | tf_op jit(solution)/shard_map/reduce_sum | solution.py:27
  237.3 130.5 %reduce-scatter.2.cloned.1.call-done = f32[128,1536]{1,0:T(8,128)} async-done(((f32[2048,1536]{1,0:T(8,128)}), f32[128,1536]{1,0:T(8,128)}) %reduce-scatter.2.cloned.1.call-update) | async-done | bytes 786448 | tf_op jit(solution)/shard_map/reduce_scatter | solution.py:15
  367.8 2.1 broadcast_multiply_fusion
  (1 shorter events, 0.0 us)
Async XLA Ops:
  7.2 50.0 %all-gather.4.cloned.1.call-start = ((), (), s32[]{:S(2)}) async-start(), calls=%async_computation.1 | async-start | bytes 4718592 | tf_op jit(solution)/shard_map/all_gather | solution.py:10
  7.9 220.9 %all-gather.6.cloned.1.call-start = ((), (), s32[]{:S(2)}) async-start(), calls=%async_computation.3 | async-start | bytes 18874368 | tf_op jit(solution)/shard_map/all_gather | solution.py:27
  76.1 1.9 copy-start
  76.2 291.7 %reduce-scatter.2.cloned.1.call-start = ((), (), s32[]{:S(2)}) async-start(), calls=%async_computation.2 | async-start | bytes 13369344 | tf_op jit(solution)/shard_map/reduce_scatter | solution.py:15
Sparse Core Ops, SparseCore 0:
  9.5 47.6 all-gather.3
  76.3 152.4 all-gather.5
  232.9 134.9 reduce-scatter.1
